TPU v7x, 512 devices: a whole 4x8x8 slice. The times are simulated.
512 devices in a mesh: kv: 8 (over x, core), seq: 64 (over z, y).
Axes of the slice: x: 4, y: 8, z: 8, core: 2. Of those that a mesh axis runs over, the one named last changes fastest.
Arguments:
- queries: bfloat16 [512, 4096], P(('kv', 'seq')), may hold values from -6 to 6
- out_grad: bfloat16 [512, 4096], P(('kv', 'seq')), may hold values from -3072 to 3072
- saved_out: bfloat16 [512, 4096], P(('kv', 'seq')), may hold values from -1.5 to 1.5
- saved_lse: float32 [512, 32], P(('kv', 'seq')), as said below
- video_keys: bfloat16 [16384, 1024], P('seq', 'kv'), may hold values from -6 to 6
- video_values: bfloat16 [16384, 1024], P('seq', 'kv'), may hold values from -6 to 6
Outputs:
- grad_queries: bfloat16 [512, 4096], P(('kv', 'seq'))
- grad_keys: bfloat16 [16384, 1024], P('seq', 'kv')
- grad_values: bfloat16 [16384, 1024], P('seq', 'kv')
Inputs may be any that keep to these rules, and one draw needn't show every extreme that they name: saved_lse lies between log(16384) and log(16384) + 1.5.
All inputs are finite; a program needn't handle non-finite values.
Results may differ from a plain program's by a relative error of at most 0.0057.
Values may be sent and summed in bfloat16 or wider, within the bound.
A program may use at most 64 MiB of HBM per device.

v0:
```python
import math
import jax
import jax.numpy as jnp
from jax import lax
from jax.sharding import PartitionSpec as P


def head_columns(block, first, width):
    return lax.dynamic_slice_in_dim(block, first, width, 1)


def seq_major(block, kv_count, seq_count):
    total_rows = block.shape[0]
    width = block.shape[1]
    shaped = block.reshape(kv_count, seq_count, total_rows // (kv_count * seq_count), width)
    return shaped.transpose(1, 0, 2, 3).reshape(total_rows, width)


def make_accumulate(
    lse_group,
    delta_group,
    group_index,
    group_width,
    group_heads,
    head_width,
    score_scale,
    video_keys,
    video_values,
):

    def accumulate(totals, pieces, offset):
        key_total, value_total, query_rows = totals
        query_block, grad_block = pieces
        query_block = head_columns(query_block, group_index * group_width, group_width)
        grad_block = head_columns(grad_block, group_index * group_width, group_width)
        columns = []
        for member in range(group_heads):
            query_head = query_block[:, member * head_width : (member + 1) * head_width]
            grad_head = grad_block[:, member * head_width : (member + 1) * head_width]
            scores = (
                jnp.einsum("nd,kd->nk", query_head, video_keys, preferred_element_type=jnp.float32)
                * score_scale
            )
            probs = jnp.exp(scores - lse_group[:, member : member + 1])
            probs_half = probs.astype(jnp.bfloat16)
            value_total = value_total + jnp.einsum(
                "nk,nd->kd", probs_half, grad_head, preferred_element_type=jnp.float32
            )
            dprobs = jnp.einsum(
                "nd,kd->nk", grad_head, video_values, preferred_element_type=jnp.float32
            )
            dscores = (probs * (dprobs - delta_group[:, member : member + 1])).astype(jnp.bfloat16)
            key_total = key_total + jnp.einsum(
                "nk,nd->kd", dscores, query_head, preferred_element_type=jnp.float32
            )
            columns.append(
                jnp.einsum("nk,kd->nd", dscores, video_keys, preferred_element_type=jnp.float32)
            )
        query_rows = jnp.concatenate(columns, axis=1)
        return (key_total, value_total, query_rows)

    return accumulate


def shards(queries, out_grad, saved_out, saved_lse, video_keys, video_values):
    kv_count = lax.axis_size("kv")
    seq_count = lax.axis_size("seq")
    group_index = lax.axis_index("kv")
    head_width = video_keys.shape[1]
    group_heads = saved_lse.shape[1] // kv_count
    group_width = group_heads * head_width
    own_rows = queries.shape[0]
    total_rows = own_rows * kv_count * seq_count
    score_scale = 1.0 / math.sqrt(head_width)
    products = out_grad.astype(jnp.float32) * saved_out.astype(jnp.float32)
    own_delta = products.reshape(own_rows, -1, head_width).sum(axis=2)
    lse_all, delta_all = (
        lax.all_gather(saved_lse, ("kv", "seq"), axis=0, tiled=True),
        lax.all_gather(own_delta, ("kv", "seq"), axis=0, tiled=True),
    )
    lse_wide = head_columns(lse_all, group_index * group_heads, group_heads)
    delta_wide = head_columns(delta_all, group_index * group_heads, group_heads)
    key_rows = video_keys.shape[0]
    initial = (
        jnp.zeros((key_rows, head_width), jnp.float32),
        jnp.zeros((key_rows, head_width), jnp.float32),
        jnp.zeros((total_rows, group_width), jnp.float32),
    )
    wide_step = make_accumulate(
        lse_wide,
        delta_wide,
        group_index,
        group_width,
        group_heads,
        head_width,
        score_scale,
        video_keys,
        video_values,
    )
    gathered = (
        lax.all_gather(queries, ("kv", "seq"), axis=0, tiled=True),
        lax.all_gather(out_grad, ("kv", "seq"), axis=0, tiled=True),
    )
    key_total, value_total, query_rows = wide_step(initial, gathered, 0)
    query_rows = seq_major(query_rows, kv_count, seq_count)
    summed = lax.psum_scatter(
        query_rows.reshape(seq_count, total_rows // seq_count, group_width),
        "seq",
        scatter_dimension=0,
        tiled=True,
    )
    rounded = (summed * score_scale).astype(jnp.bfloat16).reshape(kv_count, own_rows, group_width)
    returned = lax.all_to_all(rounded, "kv", split_axis=0, concat_axis=2, tiled=True)
    grad_queries = returned.reshape(own_rows, kv_count * group_width)
    return (
        grad_queries,
        (key_total * score_scale).astype(jnp.bfloat16),
        value_total.astype(jnp.bfloat16),
    )


def solution(mesh):
    return jax.shard_map(
        shards,
        mesh=mesh,
        in_specs=(
            P(("kv", "seq"), None),
            P(("kv", "seq"), None),
            P(("kv", "seq"), None),
            P(("kv", "seq"), None),
            P("seq", "kv"),
            P("seq", "kv"),
        ),
        out_specs=(P(("kv", "seq"), None), P("seq", "kv"), P("seq", "kv")),
        check_vma=False,
    )
```

profile of v0, /device:TPU:1, one launch (start us, length us, event | category | flops | bytes accessed | tf_op | source)
XLA Modules:
  0.0 824.8 jit_solution(11572126414588842598)
XLA Ops:
  7.2 0.8 convert_multiply_fusion
  8.1 0.3 dynamic-update-slice
  8.4 0.8 reshape.27
  9.3 0.7 all-gather.7.cloned.1.call-update
  10.1 0.7 all-gather.9.cloned.1.call-update
  10.8 66.6 %all-gather.2 = f32[512,1,32]{2,1,0:T(1,128)S(1)} all-gather(f32[1,1,32]{2,1,0:T(1,128)} %bitcast.70), channel_id=1, replica_groups=mesh['kv'=8,'seq'=64] {'kv','seq'}, dimensions={0}, use_global_device_ids=true | all-gather | bytes 65664 | tf_op jit(solution)/shard_map/all_gather | solution.py:78
  77.4 0.6 constant_dynamic-slice_fusion.1
  78.1 212.3 %all-reduce.5.cloned.1.call-done = f32[512,32]{1,0:T(8,128)} async-done(((f32[512,32]{1,0:T(8,128)}), f32[512,32]{1,0:T(8,128)}) %all-reduce.5.cloned.1.call-update) | async-done | bytes 65552
  290.5 2.0 dynamic-slice_reduce_fusion.3
  292.5 127.6 %all-gather.7.cloned.1.call-done = bf16[512,1,4096]{2,1,0:T(2,128)(2,1)} async-done(((bf16[1,1,4096]{2,1,0:T(2,128)(2,1)}), bf16[512,1,4096]{2,1,0:T(2,128)(2,1)}) %all-gather.7.cloned.1.call-update) | async-done | bytes 4194320 | tf_op jit(solution)/shard_map/all_gather | solution.py:101
  420.0 2.3 constant_dynamic-slice_fusion.2
  422.3 0.1 copy.24
  422.5 126.2 %all-gather.9.cloned.1.call-done = bf16[512,1,4096]{2,1,0:T(2,128)(2,1)} async-done(((bf16[1,1,4096]{2,1,0:T(2,128)(2,1)}), bf16[512,1,4096]{2,1,0:T(2,128)(2,1)}) %all-gather.9.cloned.1.call-update) | async-done | bytes 4194320 | tf_op jit(solution)/shard_map/all_gather | solution.py:102
  548.7 2.3 constant_dynamic-slice_fusion
  551.0 0.1 copy.23
  551.1 0.2 fusion.10
  551.4 0.2 fusion.12
  551.6 0.2 fusion.46
  551.8 0.2 fusion.7
  552.1 0.2 fusion.13
  552.3 0.2 fusion.45
  552.6 0.2 fusion.4
  552.8 0.2 fusion.14
  553.1 0.2 fusion.44
  553.3 0.4 copy-done.2
  553.8 0.2 fusion.1
  554.0 0.2 fusion.15
  554.3 0.7 copy-done.3
  555.0 0.2 fusion.43
  555.2 1.1 pad_maximum_fusion
  556.3 2.6 copy.16
  558.9 2.8 copy.17
  561.7 1.2 fusion.38
  562.9 1.2 convolution_add_fusion.5
  564.2 1.9 convolution_add_fusion.4
  566.0 0.3 fusion.22
  566.3 0.3 convolution_add_fusion.2
  566.6 0.3 convolution_add_fusion.1
  566.8 0.9 fusion.18
  567.7 233.1 %reduce-scatter.4.cloned.1.call-done = f32[1,8,512]{2,1,0:T(8,128)} async-done(((f32[64,8,512]{2,1,0:T(8,128)}), f32[1,8,512]{2,1,0:T(8,128)}) %reduce-scatter.4.cloned.1.call-update) | async-done | bytes 16400
  800.9 0.7 fusion.41
  801.6 0.5 broadcast.13
  802.1 0.6 reduce.9
  802.8 0.6 reshape.44
  803.4 9.7 %all-to-all-start = ((bf16[8,2,256]{2,1,0:T(2,128)(2,1)}), bf16[8,2,256]{2,1,0:T(2,128)(2,1)S(1)}, u32[]{:S(2)}, u32[]{:S(2)}) async-start(bf16[8,2,256]{2,1,0:T(2,128)(2,1)} %reshape.44), calls=%async_computation | async-start | bytes 16384 | tf_op jit(solution)/shard_map/all_to_all | solution.py:113
  813.0 1.8 fusion.17
  814.9 2.8 all-to-all-done
  817.7 0.6 reshape.45
  (18 shorter events, 0.5 us)
Async XLA Ops:
  7.2 543.9 %copy-start = (bf16[256,128]{1,0:T(8,128)(2,1)S(1)}, bf16[256,128]{1,0:T(8,128)(2,1)}, u32[]{:S(2)}) copy-start(bf16[256,128]{1,0:T(8,128)(2,1)} %param.10) | copy-start | bytes 196612
  7.2 544.2 %copy-start.4 = (bf16[256,128]{1,0:T(8,128)(2,1)S(1)}, bf16[256,128]{1,0:T(8,128)(2,1)}, u32[]{:S(2)}) copy-start(bf16[256,128]{1,0:T(8,128)(2,1)} %param.11) | copy-start | bytes 196612
  7.2 283.3 %all-reduce.5.cloned.1.call-start = ((), (), s32[]{:S(2)}) async-start(), calls=%async_computation.4 | async-start | bytes 524288
  9.3 410.8 %all-gather.7.cloned.1.call-start = ((), (), s32[]{:S(2)}) async-start(), calls=%async_computation.2 | async-start | bytes 8404992 | tf_op jit(solution)/shard_map/all_gather | solution.py:101
  10.0 538.6 %all-gather.9.cloned.1.call-start = ((), (), s32[]{:S(2)}) async-start(), calls=%async_computation.3 | async-start | bytes 8404992 | tf_op jit(solution)/shard_map/all_gather | solution.py:102
  10.7 790.1 %reduce-scatter.4.cloned.1.call-start = ((), (), s32[]{:S(2)}) async-start(), calls=%async_computation.5 | async-start | bytes 1064960
  552.3 1.0 copy-start.1
  553.1 0.7 copy-start.2
  554.3 0.7 copy-start.3
  803.4 14.3 %all-to-all-start = ((bf16[8,2,256]{2,1,0:T(2,128)(2,1)}), bf16[8,2,256]{2,1,0:T(2,128)(2,1)S(1)}, u32[]{:S(2)}, u32[]{:S(2)}) async-start(bf16[8,2,256]{2,1,0:T(2,128)(2,1)} %reshape.44), calls=%async_computation | async-start | bytes 16384 | tf_op jit(solution)/shard_map/all_to_all | solution.py:113
Sparse Core Ops, SparseCore 0:
  13.0 277.4 all-reduce.4
  294.9 125.1 all-gather.6
  424.5 124.1 all-gather.8
  561.8 239.0 reduce-scatter.3
where the time goes:
time: 825 us
  waiting for transfers between devices  703 us (85%)
  blocking collectives  66.6 us (8%)
  local copies, waits for them, and re-layouts  17 us (2%)
  between operations  14 us (2%)
  matrix products  10.7 us (1%)
  starting transfers between devices  9.82 us (1%)
    unnamed x6, waiting for transfers between devices  447 us
    all_gather x1, waiting for transfers between devices, shards(): lax.all_gather(queries, ('kv', 'seq'), axis=0, tiled=True)  128 us
    all_gather x1, waiting for transfers between devices, shards(): lax.all_gather(out_grad, ('kv', 'seq'), axis=0, tiled=True)  126 us
    all_gather x1, blocking collectives, shards(): lax.all_gather(saved_lse, ('kv', 'seq'), axis=0, tiled=True)  66.6 us
  transfers between devices with their start and end apart: 5, of which 5 were waited for; matrix products, arithmetic and copies ran while one was open for 2% of the time, Pallas kernels for 0%

commit v1 on v0

--- a/solution.py
+++ b/solution.py
@@ -98,7 +98,12 @@
         video_values,
     )
     gathered = (
-        lax.all_gather(queries, ("kv", "seq"), axis=0, tiled=True),
+        jnp.concatenate(
+            lax.all_to_all(
+                jnp.stack([queries] * lax.axis_size(("kv", "seq"))), ("kv", "seq"), 0, 0
+            ),
+            axis=0,
+        ),
         lax.all_gather(out_grad, ("kv", "seq"), axis=0, tiled=True),
     )
     key_total, value_total, query_rows = wide_step(initial, gathered, 0)

time: 825 us -> 779 us (0.944)
  waiting for transfers between devices: 703 us -> 487 us
  blocking collectives: 66.6 us -> 144 us
  local copies, waits for them, and re-layouts: 17 us -> 56.1 us
  other arithmetic: 3.31 us -> 31.5 us
  starting transfers between devices: 9.82 us -> 34.1 us
    all_gather x1 -> x0, waiting for transfers between devices: 128 us -> none  [shards(): lax.all_gather(queries, ('kv', 'seq'), axis=0, tiled=True)]
    unnamed x6 -> x5, waiting for transfers between devices: 447 us -> 357 us
    all_gather x1, blocking collectives: 66.6 us -> 144 us  [shards(): lax.all_gather(saved_lse, ('kv', 'seq'), axis=0, tiled=True)]
    unnamed x16 -> x20, local copies, waits for them, and re-layouts: 2.92 us -> 36.5 us
    another operation x0 -> x1, other arithmetic: none -> 27.4 us  [shards(): jnp.stack([queries] * lax.axis_size(('kv', 'seq')))]
    all_to_all x0 -> x1, starting transfers between devices: none -> 24.2 us  [shards(): lax.all_to_all(jnp.stack([queries] * lax.axis_size(('kv', 'seq'))), ('kv'...]
  transfers between devices with their start and end apart: 5 -> 5, of which waited for: 5 -> 4; matrix products, arithmetic and copies ran while one was open for 2% -> 7% of each run, Pallas kernels for 0% -> 0%
where the time goes in v1:
time: 779 us; the launch traced here: 777 us
  waiting for transfers between devices  487 us (63%)
  blocking collectives  144 us (18%)
  local copies, waits for them, and re-layouts  56.1 us (7%)
  starting transfers between devices  34.1 us (4%)
  other arithmetic  31.5 us (4%)
  between operations  14 us (2%)
  matrix products  10.6 us (1%)
    unnamed x5, waiting for transfers between devices  357 us
    all_gather x1, blocking collectives, shards(): lax.all_gather(saved_lse, ('kv', 'seq'), axis=0, tiled=True)  144 us
    all_gather x1, waiting for transfers between devices, shards(): lax.all_gather(out_grad, ('kv', 'seq'), axis=0, tiled=True)  128 us
    unnamed x20, local copies, waits for them, and re-layouts  36.5 us
    another operation x1, other arithmetic, shards(): jnp.stack([queries] * lax.axis_size(('kv', 'seq')))  27.4 us
    all_to_all x1, starting transfers between devices, shards(): lax.all_to_all(jnp.stack([queries] * lax.axis_size(('kv', 'seq'))), ('kv'...  24.2 us
  transfers between devices with their start and end apart: 5, of which 4 were waited for; matrix products, arithmetic and copies ran while one was open for 7% of the time, Pallas kernels for 0%

profile of v1, /device:TPU:1, one launch (start us, length us, event | category | flops | bytes accessed | tf_op | source)
XLA Modules:
  0.0 777.1 jit_solution(12828912137582704239)
XLA Ops:
  7.2 0.8 convert_multiply_fusion
  8.1 0.3 dynamic-update-slice
  8.4 0.8 reshape.32
  9.3 0.7 all-gather.5.cloned.1.call-update
  10.0 0.8 reduce.1
  10.8 5.6 stack.2
  16.4 0.5 broadcast.17
  16.9 27.4 %reduce.10 = bf16[512,4096]{1,0:T(8,128)(2,1)} reduce(bf16[512,1,4096]{2,1,0:T(2,128)(2,1)} %stack.2, bf16[]{:T(256)} %broadcast.17), dimensions={1}, to_apply=%stack.2.reduce_sub_computation | reduce | bytes 8388610 | tf_op jit(solution)/shard_map/stack | solution.py:103
  44.3 7.9 %reshape.47 = bf16[512,2,2048]{2,1,0:T(2,128)(2,1)} reshape(bf16[512,4096]{1,0:T(8,128)(2,1)} %reduce.10) | data formatting | bytes 8388608
  52.1 24.2 %all-to-all-start = ((bf16[512,2,2048]{2,1,0:T(2,128)(2,1)}), bf16[512,2,2048]{2,1,0:T(2,128)(2,1)}, u32[]{:S(2)}, u32[]{:S(2)}) async-start(bf16[512,2,2048]{2,1,0:T(2,128)(2,1)} %reshape.47), calls=%async_computation | async-start | bytes 8388608 | tf_op jit(solution)/shard_map/all_to_all | solution.py:102
  76.4 143.6 %all-gather.1 = f32[512,1,32]{2,1,0:T(1,128)S(1)} all-gather(f32[1,1,32]{2,1,0:T(1,128)S(1)} %bitcast.68), channel_id=1, replica_groups=mesh['kv'=8,'seq'=64] {'kv','seq'}, dimensions={0}, use_global_device_ids=true | all-gather | bytes 65664 | tf_op jit(solution)/shard_map/all_gather | solution.py:78
  220.1 0.6 constant_dynamic-slice_fusion.1
  220.8 122.8 %all-reduce.5.cloned.1.call-done = f32[512,32]{1,0:T(8,128)} async-done(((f32[512,32]{1,0:T(8,128)}), f32[512,32]{1,0:T(8,128)}) %all-reduce.5.cloned.1.call-update) | async-done | bytes 65552
  343.6 1.9 dynamic-slice_reduce_fusion.3
  345.6 127.6 %all-gather.5.cloned.1.call-done = bf16[512,1,4096]{2,1,0:T(2,128)(2,1)} async-done(((bf16[1,1,4096]{2,1,0:T(2,128)(2,1)}), bf16[512,1,4096]{2,1,0:T(2,128)(2,1)}) %all-gather.5.cloned.1.call-update) | async-done | bytes 4194320 | tf_op jit(solution)/shard_map/all_gather | solution.py:107
  473.2 2.3 constant_dynamic-slice_fusion
  475.7 26.6 %reshape.48 = bf16[512,1,4096]{2,1,0:T(2,128)(2,1)} reshape(bf16[512,2,2048]{2,1,0:T(2,128)(2,1)} %all-to-all-done) | data formatting | bytes 8388608
  502.3 2.3 constant_dynamic-slice_fusion.2
  504.7 0.2 fusion.1
  505.0 0.2 fusion.4
  505.2 0.2 fusion.7
  505.5 0.2 fusion.10
  505.7 0.2 fusion.15
  506.0 0.2 fusion.43
  506.2 0.2 fusion.14
  506.5 0.2 fusion.44
  506.7 0.2 fusion.13
  507.0 0.2 fusion.45
  507.2 0.2 fusion.12
  507.5 0.2 copy-done.3
  507.9 1.1 pad_maximum_fusion
  509.0 2.6 copy.16
  511.6 2.8 copy.17
  514.4 1.2 fusion.38
  515.6 1.2 convolution_add_fusion.5
  516.9 1.9 convolution_add_fusion.4
  518.7 0.3 fusion.22
  519.0 0.3 convolution_add_fusion.2
  519.3 0.3 convolution_add_fusion.1
  519.5 0.9 fusion.18
  520.4 233.1 %reduce-scatter.4.cloned.1.call-done = f32[1,8,512]{2,1,0:T(8,128)} async-done(((f32[64,8,512]{2,1,0:T(8,128)}), f32[1,8,512]{2,1,0:T(8,128)}) %reduce-scatter.4.cloned.1.call-update) | async-done | bytes 16400
  753.5 0.7 fusion.41
  754.3 0.6 reduce.11
  754.9 0.6 reshape.49
  755.5 9.8 %all-to-all-start.1 = ((bf16[8,2,256]{2,1,0:T(2,128)(2,1)}), bf16[8,2,256]{2,1,0:T(2,128)(2,1)S(1)}, u32[]{:S(2)}, u32[]{:S(2)}) async-start(bf16[8,2,256]{2,1,0:T(2,128)(2,1)} %reshape.49), calls=%async_computation.1 | async-start | bytes 16384 | tf_op jit(solution)/shard_map/all_to_all | solution.py:118
  765.3 1.8 fusion.17
  767.1 2.8 all-to-all-done.1
  769.9 0.6 reshape.50
  (24 shorter events, 0.9 us)
Async XLA Ops:
  7.2 497.5 %copy-start = (bf16[256,128]{1,0:T(8,128)(2,1)S(1)}, bf16[256,128]{1,0:T(8,128)(2,1)}, u32[]{:S(2)}) copy-start(bf16[256,128]{1,0:T(8,128)(2,1)} %param.10) | copy-start | bytes 196612
  7.2 336.5 %all-reduce.5.cloned.1.call-start = ((), (), s32[]{:S(2)}) async-start(), calls=%async_computation.4 | async-start | bytes 524288
  9.2 464.0 %all-gather.5.cloned.1.call-start = ((), (), s32[]{:S(2)}) async-start(), calls=%async_computation.3 | async-start | bytes 8404992 | tf_op jit(solution)/shard_map/all_gather | solution.py:107
  44.3 32.1 %copy-start.5 = (f32[1,32]{1,0:T(1,128)S(1)}, f32[1,32]{1,0:T(1,128)}, u32[]{:S(2)}) copy-start(f32[1,32]{1,0:T(1,128)} %param.9) | copy-start | bytes 388
  52.1 423.5 %all-to-all-start = ((bf16[512,2,2048]{2,1,0:T(2,128)(2,1)}), bf16[512,2,2048]{2,1,0:T(2,128)(2,1)}, u32[]{:S(2)}, u32[]{:S(2)}) async-start(bf16[512,2,2048]{2,1,0:T(2,128)(2,1)} %reshape.47), calls=%async_computation | async-start | bytes 8388608 | tf_op jit(solution)/shard_map/all_to_all | solution.py:102
  76.4 677.2 %reduce-scatter.4.cloned.1.call-start = ((), (), s32[]{:S(2)}) async-start(), calls=%async_computation.5 | async-start | bytes 1064960
  475.7 30.1 %copy-start.4 = (bf16[256,128]{1,0:T(8,128)(2,1)S(1)}, bf16[256,128]{1,0:T(8,128)(2,1)}, u32[]{:S(2)}) copy-start(bf16[256,128]{1,0:T(8,128)(2,1)} %param.11) | copy-start | bytes 196612
  506.0 1.2 copy-start.1
  506.5 0.7 copy-start.2
  507.0 0.7 copy-start.3
  755.5 14.4 %all-to-all-start.1 = ((bf16[8,2,256]{2,1,0:T(2,128)(2,1)}), bf16[8,2,256]{2,1,0:T(2,128)(2,1)S(1)}, u32[]{:S(2)}, u32[]{:S(2)}) async-start(bf16[8,2,256]{2,1,0:T(2,128)(2,1)} %reshape.49), calls=%async_computation.1 | async-start | bytes 16384 | tf_op jit(solution)/shard_map/all_to_all | solution.py:118
Sparse Core Ops, SparseCore 0:
  13.0 330.6 all-reduce.4
  348.1 125.1 all-gather.4
  514.5 238.9 reduce-scatter.3
